TPU v7x, 32 devices: a whole 2x2x4 slice. The times are simulated.
32 devices in a mesh: groups: 2 (over x), tm: 16 (over z, y, core).
Axes of the slice: x: 2, y: 2, z: 4, core: 2. Of those that a mesh axis runs over, the one named last changes fastest.
Arguments:
- states: bfloat16 [4096, 2, 1024], P('tm', 'groups'), parts along dimension 1, may hold values from -6 to 6
- goals: bfloat16 [4096, 2, 1024], P('tm', 'groups'), parts along dimension 1, may hold values from -6 to 6
- pos_offset: int32 [16, 2, 8], P('tm', 'groups'), parts along dimension 1, may hold values from 0 to 15
- neg_blocks: int32 [16, 2, 16], P('tm', 'groups'), parts along dimension 1, may hold values from 0 to 15
Outputs:
- loss_mean: float32 [2], P('groups'), parts along dimension 0
- grad_states: float32 [4096, 2, 1024], P('tm', 'groups'), parts along dimension 1
- grad_goals: float32 [4096, 2, 1024], P('tm', 'groups'), parts along dimension 1
There are 2 independent parts, one for each index of `groups`. A program takes and returns all parts, laid end to end along the dimension named above; each array names one. Nothing has to cross between parts.
All inputs are finite; a program needn't handle non-finite values.
Results may differ from a plain program's by a relative error of at most 0.012.
Values may be sent and summed in bfloat16 or wider, within the bound.
No kernel may reach another device: no remote copies, remote signals or barrier semaphores. Data moves between devices by JAX's collectives and lax.ppermute only.
A program may use at most 128 MiB of HBM per device.

v0:
```python
import math
import jax
import jax.numpy as jnp
from jax import lax
from jax.sharding import PartitionSpec as P

E = 1024
L = 256


def pair_weights(pos_offset, neg_blocks, row_first, row_count, col_count):
    block_count = row_count // L
    row_blocks = row_first // L + jnp.arange(block_count, dtype=jnp.int32)
    col_times = jnp.arange(col_count, dtype=jnp.int32)
    col_blocks = col_times // L
    targets = row_blocks[:, None, None] + pos_offset
    pos_count = jnp.sum((targets[..., None] == col_blocks).astype(jnp.float32), axis=2)
    neg_count = jnp.sum((neg_blocks[..., None] == col_blocks).astype(jnp.float32), axis=2)
    pos_count = jnp.repeat(jnp.swapaxes(pos_count, 0, 1), L, axis=1)
    neg_count = jnp.repeat(jnp.swapaxes(neg_count, 0, 1), L, axis=1)
    row_times = row_first + jnp.arange(row_count, dtype=jnp.int32)
    later_mask = (col_times[None, :] > row_times[:, None]).astype(jnp.float32)
    return (pos_count * later_mask, neg_count)


def score_terms(anchor_rows, goal_rows, pos_weight, neg_weight):
    inv_root = 1.0 / math.sqrt(E)
    scores = (
        jnp.einsum("qte,kte->tqk", anchor_rows, goal_rows, preferred_element_type=jnp.float32)
        * inv_root
    )
    loss_sum = jnp.sum(pos_weight * jax.nn.softplus(-scores) + neg_weight * jax.nn.softplus(scores))
    slopes = neg_weight * jax.nn.sigmoid(scores) - pos_weight * jax.nn.sigmoid(-scores)
    return (loss_sum, (slopes * inv_root).astype(jnp.bfloat16))


def per_device(states, goals, pos_offset, neg_blocks):
    row_count = states.shape[0]
    traj_count = states.shape[1]
    steps_all = row_count * lax.axis_size("tm")
    row_first = lax.axis_index("tm") * row_count
    goal_piece = lax.all_gather(goals, "tm", axis=0, tiled=True)
    col_count = goal_piece.shape[0]
    pos_weight, neg_weight = pair_weights(pos_offset, neg_blocks, row_first, row_count, col_count)
    loss_sum, coeffs = score_terms(states, goal_piece, pos_weight, neg_weight)
    grad_rows = jnp.einsum("tqk,kte->qte", coeffs, goal_piece, preferred_element_type=jnp.float32)
    loss_sum, coeffs, grad_rows = (loss_sum, coeffs, grad_rows)
    folded = (grad_rows, loss_sum, coeffs)
    grad_states = folded[0]
    loss_sum = folded[1]
    coeff_all = folded[2]
    grad_goals = lax.psum_scatter(
        jnp.einsum("tqk,qte->kte", coeff_all, states, preferred_element_type=jnp.float32).astype(
            jnp.bfloat16
        ),
        "tm",
        scatter_dimension=0,
        tiled=True,
    ).astype(jnp.float32)
    loss_all = lax.psum(loss_sum, "tm")
    loss_mean = (loss_all / (traj_count * steps_all)).reshape(1)
    return (loss_mean, grad_states, grad_goals)


def solution(mesh):
    in_specs = (
        P("tm", "groups", None),
        P("tm", "groups", None),
        P("tm", "groups", None),
        P("tm", "groups", None),
    )
    out_specs = (P("groups"), P("tm", "groups", None), P("tm", "groups", None))
    return jax.shard_map(
        per_device, mesh=mesh, in_specs=in_specs, out_specs=out_specs, check_vma=False
    )
```

profile of v0, /device:TPU:0, one launch (start us, length us, event | category | flops | bytes accessed | tf_op | source)
XLA Modules:
  0.0 219.8 jit_solution(17836653208547374864)
XLA Ops:
  7.2 0.0 copy-start
  7.2 0.0 all-gather.2.cloned.1.call-start
  7.2 0.7 all-gather.2.cloned.1.call-update
  7.9 0.0 reduce-scatter.2.cloned.1.call-start
  8.0 0.7 add_bitcast_fusion
  8.7 0.1 convert_reduce_fusion.1
  8.8 0.8 convert_reduce_fusion
  9.6 77.6 %all-gather.2.cloned.1.call-done = bf16[4096,1,1024]{2,0,1:T(8,128)(2,1)} async-done(((bf16[256,1,1024]{2,0,1:T(8,128)(2,1)}), bf16[4096,1,1024]{2,0,1:T(8,128)(2,1)}) %all-gather.2.cloned.1.call-update) | async-done | bytes 8388624 | tf_op jit(solution)/shard_map/all_gather | solution.py:42
  87.2 0.0 copy-done
  87.2 11.5 %fusion.8 = (f32[]{:T(128)}, f32[256,4096]{1,0:T(8,128)S(1)}) fusion(f32[4096]{0:T(1024)S(1)} %convert_reduce_fusion, f32[4096]{0:T(1024)S(1)} %convert_reduce_fusion.1, s32[256]{0:T(256)S(1)} %iota_add_fusion, bf16[4096,1,1024]{2,0,1:T(8,128)(2,1)} %all-gather.2.cloned.1.call-done, bf16[256,1,1024]{2,0,1:T(8,128)(2,1)S(1)} %copy-done), kind=kOutput, calls=%fused_computation.11 | convolution fusion | flops 2168455168 | bytes 13140996 | tf_op jit(solution)/shard_map/qte,kte->tqk/dot_general | solution.py:29
  98.7 0.0 copy-start.1
  98.7 1.9 copy-done.1
  100.6 6.2 %convert_bitcast_fusion = bf16[4096,1,1024]{2,0,1:T(8,128)(2,1)} fusion(bf16[256,1,1024]{2,0,1:T(8,128)(2,1)S(1)} %copy-done, f32[256,4096]{1,0:T(8,128)S(1)} %get-tuple-element.10, f32[4096]{0:T(1024)S(1)} %convert_reduce_fusion, f32[4096]{0:T(1024)S(1)} %convert_reduce_fusion.1, s32[256]{0:T(256)S(1)} %iota_add_fusion), kind=kOutput, calls=%fused_computation.6 | convolution fusion | flops 2164260864 | bytes 13140992 | tf_op jit(solution)/shard_map/tqk,qte->kte/dot_general | solution.py:53
  106.8 0.0 reduce-scatter.2.cloned.1.call-update
  106.8 32.1 %psum.7 = f32[]{:T(128)} all-reduce(f32[]{:T(128)} %get-tuple-element.9), channel_id=1, replica_groups=mesh['groups'=2,'tm'=16] {'tm'}, use_global_device_ids=true, to_apply=%region_3.4 | all-reduce | flops 1 | bytes 8 | tf_op jit(solution)/shard_map/psum | solution.py:60
  138.9 8.2 %fusion.13 = f32[256,1,1024]{2,0,1:T(8,128)S(1)} fusion(bf16[4096,1,1024]{2,0,1:T(8,128)(2,1)} %all-gather.2.cloned.1.call-done, f32[256,4096]{1,0:T(8,128)} %copy-done.1, f32[4096]{0:T(1024)S(1)} %convert_reduce_fusion, f32[4096]{0:T(1024)S(1)} %convert_reduce_fusion.1, s32[256]{0:T(256)S(1)} %iota_add_fusion), kind=kOutput, calls=%fused_computation.18 | convolution fusion | flops 2160066560 | bytes 13665280 | tf_op jit(solution)/shard_map/tqk,kte->qte/dot_general | solution.py:46
  147.1 2.0 copy.9
  149.8 59.2 %reduce-scatter.2.cloned.1.call-done = bf16[256,1,1024]{2,0,1:T(8,128)(2,1)} async-done(((bf16[4096,1,1024]{2,0,1:T(8,128)(2,1)}), bf16[256,1,1024]{2,0,1:T(8,128)(2,1)}) %reduce-scatter.2.cloned.1.call-update) | async-done | bytes 524304 | tf_op jit(solution)/shard_map/reduce_scatter | solution.py:52
  209.0 2.8 %copy.10 = f32[256,1,1024]{2,1,0:T(1,128)} copy(bf16[256,1,1024]{2,0,1:T(8,128)(2,1)} %reduce-scatter.2.cloned.1.call-done) | data formatting | bytes 1572864
  (2 shorter events, 0.0 us)
Async XLA Ops:
  7.2 80.0 %copy-start = (bf16[256,1,1024]{2,0,1:T(8,128)(2,1)S(1)}, bf16[256,1,1024]{2,0,1:T(8,128)(2,1)}, u32[]{:S(2)}) copy-start(bf16[256,1,1024]{2,0,1:T(8,128)(2,1)} %param.4) | copy-start | bytes 1572868
  7.2 80.0 %all-gather.2.cloned.1.call-start = ((), (), s32[]{:S(2)}) async-start(), calls=%async_computation.1 | async-start | bytes 8912896 | tf_op jit(solution)/shard_map/all_gather | solution.py:42
  7.9 201.1 %reduce-scatter.2.cloned.1.call-start = ((), (), s32[]{:S(2)}) async-start(), calls=%async_computation.2 | async-start | bytes 8912896 | tf_op jit(solution)/shard_map/reduce_scatter | solution.py:52
  98.7 1.9 copy-start.1
Sparse Core Ops, SparseCore 0:
  10.2 77.0 all-gather.1
  107.0 102.0 reduce-scatter.1
where the time goes:
time: 220 us
  waiting for transfers between devices  138 us (63%)
  blocking collectives  32.1 us (15%)
  matrix products  25.9 us (12%)
  between operations  15.9 us (7%)
  local copies, waits for them, and re-layouts  6.8 us (3%)
    all_gather x1, waiting for transfers between devices, per_device(): goal_piece = lax.all_gather(goals, 'tm', axis=0, tiled=True)  77.6 us
    reduce_scatter x1, waiting for transfers between devices, per_device(): lax.psum_scatter(jnp.einsum('tqk,qte->kte', coeff_all, states, preferred_...  59.2 us
    psum x1, blocking collectives, per_device(): loss_all = lax.psum(loss_sum, 'tm')  32.1 us
    dot_general x1, matrix products, score_terms(): jnp.einsum('qte,kte->tqk', anchor_rows, goal_rows, preferred_element_type...  11.5 us
    dot_general x1, matrix products, per_device(): jnp.einsum('tqk,kte->qte', coeffs, goal_piece, preferred_element_type=jnp...  8.22 us
    unnamed x6, local copies, waits for them, and re-layouts  6.8 us
    dot_general x1, matrix products, per_device(): jnp.einsum('tqk,qte->kte', coeff_all, states, preferred_element_type=jnp....  6.2 us
  transfers between devices with their start and end apart: 2, of which 2 were waited for; matrix products, arithmetic and copies ran while one was open for 5% of the time, Pallas kernels for 0%

commit v1 on v0

--- a/solution.py
+++ b/solution.py
@@ -39,7 +39,12 @@
     traj_count = states.shape[1]
     steps_all = row_count * lax.axis_size("tm")
     row_first = lax.axis_index("tm") * row_count
-    goal_piece = lax.all_gather(goals, "tm", axis=0, tiled=True)
+    ring = [goals]
+    for hop in range(15):
+        ring.append(lax.ppermute(ring[-1], "tm", [(dev, (dev + 1) % 16) for dev in range(16)]))
+    goal_piece = jnp.roll(
+        jnp.concatenate(ring[::-1], axis=0), (lax.axis_index("tm") + 1) * ring[0].shape[0], axis=0
+    )
     col_count = goal_piece.shape[0]
     pos_weight, neg_weight = pair_weights(pos_offset, neg_blocks, row_first, row_count, col_count)
     loss_sum, coeffs = score_terms(states, goal_piece, pos_weight, neg_weight)

time: 220 us -> 330 us (1.50)
  waiting for transfers between devices: 138 us -> 229 us
  local copies, waits for them, and re-layouts: 6.8 us -> 27.5 us
    ppermute x0 -> x15, waiting for transfers between devices: none -> 169 us  [per_device(): lax.ppermute(ring[-1], 'tm', [(dev, (dev + 1) % 16) for dev in range(16)])]
    all_gather x1 -> x0, waiting for transfers between devices: 77.6 us -> none  [per_device(): goal_piece = lax.all_gather(goals, 'tm', axis=0, tiled=True)]
    unnamed x6 -> x71, local copies, waits for them, and re-layouts: 6.8 us -> 27.5 us
  transfers between devices with their start and end apart: 2 -> 16, of which waited for: 2 -> 16; matrix products, arithmetic and copies ran while one was open for 5% -> 4% of each run, Pallas kernels for 0% -> 0%
where the time goes in v1:
time: 330 us; the launch traced here: 329 us
  waiting for transfers between devices  229 us (69%)
  blocking collectives  30.1 us (9%)
  local copies, waits for them, and re-layouts  27.5 us (8%)
  matrix products  23.2 us (7%)
  between operations  16.2 us (5%)
    ppermute x15, waiting for transfers between devices, per_device(): lax.ppermute(ring[-1], 'tm', [(dev, (dev + 1) % 16) for dev in range(16)])  169 us
    reduce_scatter x1, waiting for transfers between devices, per_device(): lax.psum_scatter(jnp.einsum('tqk,qte->kte', coeff_all, states, preferred_...  60.2 us
    psum x1, blocking collectives, per_device(): loss_all = lax.psum(loss_sum, 'tm')  30.1 us
    unnamed x71, local copies, waits for them, and re-layouts  27.5 us
    dot_general x1, matrix products, score_terms(): jnp.einsum('qte,kte->tqk', anchor_rows, goal_rows, preferred_element_type...  10.9 us
    dot_general x1, matrix products, per_device(): jnp.einsum('tqk,kte->qte', coeffs, goal_piece, preferred_element_type=jnp...  6.71 us
  transfers between devices with their start and end apart: 16, of which 16 were waited for; matrix products, arithmetic and copies ran while one was open for 4% of the time, Pallas kernels for 0%

profile of v1, /device:TPU:0, one launch (start us, length us, event | category | flops | bytes accessed | tf_op | source)
XLA Modules:
  0.0 328.7 jit_solution(14806740512138797146)
XLA Ops:
  7.2 0.0 reduce-scatter.2.cloned.1.call-start
  7.2 0.5 collective-permute-start
  7.8 12.1 %collective-permute-done = bf16[256,1,1024]{2,0,1:T(8,128)(2,1)S(1)} collective-permute-done((bf16[256,1,1024]{2,0,1:T(8,128)(2,1)}, bf16[256,1,1024]{2,0,1:T(8,128)(2,1)S(1)}, u32[]{:S(2)}, u32[]{:S(2)}) %collective-permute-start) | collective-permute-done | bytes 524320 | tf_op jit(solution)/shard_map/ppermute | solution.py:44
  19.8 11.3 %collective-permute-done.1 = bf16[256,1,1024]{2,0,1:T(8,128)(2,1)S(1)} collective-permute-done((bf16[256,1,1024]{2,0,1:T(8,128)(2,1)S(1)}, bf16[256,1,1024]{2,0,1:T(8,128)(2,1)S(1)}, u32[]{:S(2)}, u32[]{:S(2)}) %collective-permute-start.1) | collective-permute-done | bytes 524320 | tf_op jit(solution)/shard_map/ppermute | solution.py:44
  31.1 11.3 %collective-permute-done.2 = bf16[256,1,1024]{2,0,1:T(8,128)(2,1)S(1)} collective-permute-done((bf16[256,1,1024]{2,0,1:T(8,128)(2,1)S(1)}, bf16[256,1,1024]{2,0,1:T(8,128)(2,1)S(1)}, u32[]{:S(2)}, u32[]{:S(2)}) %collective-permute-start.2) | collective-permute-done | bytes 524320 | tf_op jit(solution)/shard_map/ppermute | solution.py:44
  42.5 11.3 %collective-permute-done.3 = bf16[256,1,1024]{2,0,1:T(8,128)(2,1)S(1)} collective-permute-done((bf16[256,1,1024]{2,0,1:T(8,128)(2,1)S(1)}, bf16[256,1,1024]{2,0,1:T(8,128)(2,1)S(1)}, u32[]{:S(2)}, u32[]{:S(2)}) %collective-permute-start.3) | collective-permute-done | bytes 524320 | tf_op jit(solution)/shard_map/ppermute | solution.py:44
  53.8 11.3 %collective-permute-done.4 = bf16[256,1,1024]{2,0,1:T(8,128)(2,1)S(1)} collective-permute-done((bf16[256,1,1024]{2,0,1:T(8,128)(2,1)S(1)}, bf16[256,1,1024]{2,0,1:T(8,128)(2,1)S(1)}, u32[]{:S(2)}, u32[]{:S(2)}) %collective-permute-start.4) | collective-permute-done | bytes 524320 | tf_op jit(solution)/shard_map/ppermute | solution.py:44
  65.1 0.8 copy-done.3
  65.9 11.3 %collective-permute-done.5 = bf16[256,1,1024]{2,0,1:T(8,128)(2,1)S(1)} collective-permute-done((bf16[256,1,1024]{2,0,1:T(8,128)(2,1)S(1)}, bf16[256,1,1024]{2,0,1:T(8,128)(2,1)S(1)}, u32[]{:S(2)}, u32[]{:S(2)}) %collective-permute-start.5) | collective-permute-done | bytes 524320 | tf_op jit(solution)/shard_map/ppermute | solution.py:44
  77.2 0.8 copy-done.5
  78.0 11.3 %collective-permute-done.6 = bf16[256,1,1024]{2,0,1:T(8,128)(2,1)S(1)} collective-permute-done((bf16[256,1,1024]{2,0,1:T(8,128)(2,1)S(1)}, bf16[256,1,1024]{2,0,1:T(8,128)(2,1)S(1)}, u32[]{:S(2)}, u32[]{:S(2)}) %collective-permute-start.6) | collective-permute-done | bytes 524320 | tf_op jit(solution)/shard_map/ppermute | solution.py:44
  89.3 0.8 copy-done.7
  90.1 11.3 %collective-permute-done.7 = bf16[256,1,1024]{2,0,1:T(8,128)(2,1)S(1)} collective-permute-done((bf16[256,1,1024]{2,0,1:T(8,128)(2,1)S(1)}, bf16[256,1,1024]{2,0,1:T(8,128)(2,1)S(1)}, u32[]{:S(2)}, u32[]{:S(2)}) %collective-permute-start.7) | collective-permute-done | bytes 524320 | tf_op jit(solution)/shard_map/ppermute | solution.py:44
  101.4 0.8 copy-done.9
  102.2 11.3 %collective-permute-done.8 = bf16[256,1,1024]{2,0,1:T(8,128)(2,1)S(1)} collective-permute-done((bf16[256,1,1024]{2,0,1:T(8,128)(2,1)S(1)}, bf16[256,1,1024]{2,0,1:T(8,128)(2,1)S(1)}, u32[]{:S(2)}, u32[]{:S(2)}) %collective-permute-start.8) | collective-permute-done | bytes 524320 | tf_op jit(solution)/shard_map/ppermute | solution.py:44
  113.5 0.8 copy-done.11
  114.3 11.3 %collective-permute-done.9 = bf16[256,1,1024]{2,0,1:T(8,128)(2,1)S(1)} collective-permute-done((bf16[256,1,1024]{2,0,1:T(8,128)(2,1)S(1)}, bf16[256,1,1024]{2,0,1:T(8,128)(2,1)S(1)}, u32[]{:S(2)}, u32[]{:S(2)}) %collective-permute-start.9) | collective-permute-done | bytes 524320 | tf_op jit(solution)/shard_map/ppermute | solution.py:44
  125.6 0.8 copy-done.13
  126.4 11.3 %collective-permute-done.10 = bf16[256,1,1024]{2,0,1:T(8,128)(2,1)S(1)} collective-permute-done((bf16[256,1,1024]{2,0,1:T(8,128)(2,1)S(1)}, bf16[256,1,1024]{2,0,1:T(8,128)(2,1)S(1)}, u32[]{:S(2)}, u32[]{:S(2)}) %collective-permute-start.10) | collective-permute-done | bytes 524320 | tf_op jit(solution)/shard_map/ppermute | solution.py:44
  137.7 0.8 copy-done.15
  138.5 11.3 %collective-permute-done.11 = bf16[256,1,1024]{2,0,1:T(8,128)(2,1)S(1)} collective-permute-done((bf16[256,1,1024]{2,0,1:T(8,128)(2,1)S(1)}, bf16[256,1,1024]{2,0,1:T(8,128)(2,1)S(1)}, u32[]{:S(2)}, u32[]{:S(2)}) %collective-permute-start.11) | collective-permute-done | bytes 524320 | tf_op jit(solution)/shard_map/ppermute | solution.py:44
  149.8 0.8 copy-done.17
  150.6 11.4 %collective-permute-done.12 = bf16[256,1,1024]{2,0,1:T(8,128)(2,1)} collective-permute-done((bf16[256,1,1024]{2,0,1:T(8,128)(2,1)S(1)}, bf16[256,1,1024]{2,0,1:T(8,128)(2,1)}, u32[]{:S(2)}, u32[]{:S(2)}) %collective-permute-start.12) | collective-permute-done | bytes 524320 | tf_op jit(solution)/shard_map/ppermute | solution.py:44
  162.0 11.5 %collective-permute-done.13 = bf16[256,1,1024]{2,0,1:T(8,128)(2,1)} collective-permute-done((bf16[256,1,1024]{2,0,1:T(8,128)(2,1)}, bf16[256,1,1024]{2,0,1:T(8,128)(2,1)}, u32[]{:S(2)}, u32[]{:S(2)}) %collective-permute-start.13) | collective-permute-done | bytes 524320 | tf_op jit(solution)/shard_map/ppermute | solution.py:44
  173.6 0.7 add_bitcast_fusion
  174.2 0.1 convert_reduce_fusion.1
  174.4 0.8 convert_reduce_fusion
  175.1 10.0 %collective-permute-done.14 = bf16[256,1,1024]{2,0,1:T(8,128)(2,1)S(1)} collective-permute-done((bf16[256,1,1024]{2,0,1:T(8,128)(2,1)}, bf16[256,1,1024]{2,0,1:T(8,128)(2,1)S(1)}, u32[]{:S(2)}, u32[]{:S(2)}) %collective-permute-start.14) | collective-permute-done | bytes 524320 | tf_op jit(solution)/shard_map/ppermute | solution.py:44
  185.1 1.1 constant_dynamic-update-slice_fusion.30
  186.2 1.1 constant_dynamic-update-slice_fusion.29
  187.3 1.1 constant_dynamic-update-slice_fusion.28
  188.4 1.1 constant_dynamic-update-slice_fusion.27
  189.5 1.1 constant_dynamic-update-slice_fusion.26
  190.5 1.1 constant_dynamic-update-slice_fusion.25
  191.6 1.1 constant_dynamic-update-slice_fusion.24
  192.7 1.1 constant_dynamic-update-slice_fusion.23
  193.8 1.1 constant_dynamic-update-slice_fusion.22
  194.9 1.1 constant_dynamic-update-slice_fusion.21
  196.1 1.1 constant_dynamic-update-slice_fusion.16
  197.2 1.1 constant_dynamic-update-slice_fusion.14
  198.3 1.1 constant_dynamic-update-slice_fusion.13
  200.1 10.9 %fusion.16 = (bf16[256,4096]{0,1:T(8,128)(2,1)S(1)}, f32[]{:T(128)}) fusion(f32[4096]{0:T(1024)S(1)} %convert_reduce_fusion, f32[4096]{0:T(1024)S(1)} %convert_reduce_fusion.1, s32[256]{0:T(256)S(1)} %iota_add_fusion, bf16[256,1,1024]{2,0,1:T(8,128)(2,1)S(1)} %copy-done, bf16[8192,1,1024]{2,0,1:T(8,128)(2,1)S(1)} %constant_dynamic-update-slice_fusion, ...), kind=kOutput, calls=%fused_computation.17 | convolution fusion | flops 2177892352 | bytes 11043848 | tf_op jit(solution)/shard_map/qte,kte->tqk/dot_general | solution.py:29
  211.0 5.6 %convert_bitcast_fusion = bf16[4096,1,1024]{2,0,1:T(8,128)(2,1)} fusion(bf16[256,4096]{0,1:T(8,128)(2,1)S(1)} %get-tuple-element.9, bf16[256,1,1024]{2,0,1:T(8,128)(2,1)S(1)} %copy-done), kind=kOutput, calls=%fused_computation.6 | convolution fusion | flops 2151677952 | bytes 11010048 | tf_op jit(solution)/shard_map/tqk,qte->kte/dot_general | solution.py:58
  216.6 30.1 %psum.7 = f32[]{:T(128)} all-reduce(f32[]{:T(128)} %get-tuple-element.10), channel_id=1, replica_groups=mesh['groups'=2,'tm'=16] {'tm'}, use_global_device_ids=true, to_apply=%region_3.4 | all-reduce | flops 1 | bytes 8 | tf_op jit(solution)/shard_map/psum | solution.py:65
  246.7 6.7 %fusion.18 = f32[256,1,1024]{0,2,1:T(8,128)} fusion(bf16[256,4096]{0,1:T(8,128)(2,1)S(1)} %get-tuple-element.9, bf16[8192,1,1024]{2,0,1:T(8,128)(2,1)} %copy-done.1, s32[]{:T(128)S(6)} %select_n.40), kind=kOutput, calls=%fused_computation.21 | convolution fusion | flops 2147483648 | bytes 11534340 | tf_op jit(solution)/shard_map/tqk,kte->qte/dot_general | solution.py:51
  253.4 3.6 %copy.9 = f32[256,1,1024]{2,1,0:T(1,128)} copy(f32[256,1,1024]{0,2,1:T(8,128)} %fusion.18) | data formatting | bytes 2097152
  257.7 60.2 %reduce-scatter.2.cloned.1.call-done = bf16[256,1,1024]{2,0,1:T(8,128)(2,1)} async-done(((bf16[4096,1,1024]{2,0,1:T(8,128)(2,1)}), bf16[256,1,1024]{2,0,1:T(8,128)(2,1)}) %reduce-scatter.2.cloned.1.call-update) | async-done | bytes 524304 | tf_op jit(solution)/shard_map/reduce_scatter | solution.py:57
  317.9 2.8 copy.10
  (66 shorter events, 0.8 us)
Async XLA Ops:
  7.2 192.9 %copy-start = (bf16[256,1,1024]{2,0,1:T(8,128)(2,1)S(1)}, bf16[256,1,1024]{2,0,1:T(8,128)(2,1)}, u32[]{:S(2)}) copy-start(bf16[256,1,1024]{2,0,1:T(8,128)(2,1)} %param.4) | copy-start | bytes 1572868
  7.2 192.8 %copy-start.2 = (bf16[256,1,1024]{2,0,1:T(8,128)(2,1)S(1)}, bf16[256,1,1024]{2,0,1:T(8,128)(2,1)}, u32[]{:S(2)}) copy-start(bf16[256,1,1024]{2,0,1:T(8,128)(2,1)} %param.5) | copy-start | bytes 1572868
  7.2 310.7 %reduce-scatter.2.cloned.1.call-start = ((), (), s32[]{:S(2)}) async-start(), calls=%async_computation.1 | async-start | bytes 8912896 | tf_op jit(solution)/shard_map/reduce_scatter | solution.py:57
  7.2 12.6 %collective-permute-start = (bf16[256,1,1024]{2,0,1:T(8,128)(2,1)}, bf16[256,1,1024]{2,0,1:T(8,128)(2,1)S(1)}, u32[]{:S(2)}, u32[]{:S(2)}) collective-permute-start(bf16[256,1,1024]{2,0,1:T(8,128)(2,1)} %param.5), channel_id=1, source_target_pairs={{0,1},{1,2},{2,3},{3,4},{4,5},{5,6},{6,7},{7,8},{8,9},{9,10},{10,1... | collective-permute-start | bytes 1572872 | tf_op jit(solution)/shard_map/ppermute | solution.py:44
  19.8 11.3 %collective-permute-start.1 = (bf16[256,1,1024]{2,0,1:T(8,128)(2,1)S(1)}, bf16[256,1,1024]{2,0,1:T(8,128)(2,1)S(1)}, u32[]{:S(2)}, u32[]{:S(2)}) collective-permute-start(bf16[256,1,1024]{2,0,1:T(8,128)(2,1)S(1)} %collective-permute-done), channel_id=1, source_target_pairs={{0,1},{1,2},{2,3},{3,4},{4,5},{5,6},{6,7},{7,8},{8,9},{9,10},{10,1... | collective-permute-start | bytes 1572872 | tf_op jit(solution)/shard_map/ppermute | solution.py:44
  31.1 11.3 %collective-permute-start.2 = (bf16[256,1,1024]{2,0,1:T(8,128)(2,1)S(1)}, bf16[256,1,1024]{2,0,1:T(8,128)(2,1)S(1)}, u32[]{:S(2)}, u32[]{:S(2)}) collective-permute-start(bf16[256,1,1024]{2,0,1:T(8,128)(2,1)S(1)} %collective-permute-done.1), channel_id=1, source_target_pairs={{0,1},{1,2},{2,3},{3,4},{4,5},{5,6},{6,7},{7,8},{8,9},{9,10},{10,1... | collective-permute-start | bytes 1572872 | tf_op jit(solution)/shard_map/ppermute | solution.py:44
  42.4 11.3 %collective-permute-start.3 = (bf16[256,1,1024]{2,0,1:T(8,128)(2,1)S(1)}, bf16[256,1,1024]{2,0,1:T(8,128)(2,1)S(1)}, u32[]{:S(2)}, u32[]{:S(2)}) collective-permute-start(bf16[256,1,1024]{2,0,1:T(8,128)(2,1)S(1)} %collective-permute-done.2), channel_id=1, source_target_pairs={{0,1},{1,2},{2,3},{3,4},{4,5},{5,6},{6,7},{7,8},{8,9},{9,10},{10,1... | collective-permute-start | bytes 1572872 | tf_op jit(solution)/shard_map/ppermute | solution.py:44
  53.8 11.3 %collective-permute-start.4 = (bf16[256,1,1024]{2,0,1:T(8,128)(2,1)S(1)}, bf16[256,1,1024]{2,0,1:T(8,128)(2,1)S(1)}, u32[]{:S(2)}, u32[]{:S(2)}) collective-permute-start(bf16[256,1,1024]{2,0,1:T(8,128)(2,1)S(1)} %collective-permute-done.3), channel_id=1, source_target_pairs={{0,1},{1,2},{2,3},{3,4},{4,5},{5,6},{6,7},{7,8},{8,9},{9,10},{10,1... | collective-permute-start | bytes 1572872 | tf_op jit(solution)/shard_map/ppermute | solution.py:44
  65.1 0.8 copy-start.3
  65.9 11.3 %collective-permute-start.5 = (bf16[256,1,1024]{2,0,1:T(8,128)(2,1)S(1)}, bf16[256,1,1024]{2,0,1:T(8,128)(2,1)S(1)}, u32[]{:S(2)}, u32[]{:S(2)}) collective-permute-start(bf16[256,1,1024]{2,0,1:T(8,128)(2,1)S(1)} %collective-permute-done.4), channel_id=1, source_target_pairs={{0,1},{1,2},{2,3},{3,4},{4,5},{5,6},{6,7},{7,8},{8,9},{9,10},{10,1... | collective-permute-start | bytes 1572872 | tf_op jit(solution)/shard_map/ppermute | solution.py:44
  77.2 0.8 copy-start.5
  78.0 11.3 %collective-permute-start.6 = (bf16[256,1,1024]{2,0,1:T(8,128)(2,1)S(1)}, bf16[256,1,1024]{2,0,1:T(8,128)(2,1)S(1)}, u32[]{:S(2)}, u32[]{:S(2)}) collective-permute-start(bf16[256,1,1024]{2,0,1:T(8,128)(2,1)S(1)} %collective-permute-done.5), channel_id=1, source_target_pairs={{0,1},{1,2},{2,3},{3,4},{4,5},{5,6},{6,7},{7,8},{8,9},{9,10},{10,1... | collective-permute-start | bytes 1572872 | tf_op jit(solution)/shard_map/ppermute | solution.py:44
  89.3 0.8 copy-start.7
  90.1 11.3 %collective-permute-start.7 = (bf16[256,1,1024]{2,0,1:T(8,128)(2,1)S(1)}, bf16[256,1,1024]{2,0,1:T(8,128)(2,1)S(1)}, u32[]{:S(2)}, u32[]{:S(2)}) collective-permute-start(bf16[256,1,1024]{2,0,1:T(8,128)(2,1)S(1)} %collective-permute-done.6), channel_id=1, source_target_pairs={{0,1},{1,2},{2,3},{3,4},{4,5},{5,6},{6,7},{7,8},{8,9},{9,10},{10,1... | collective-permute-start | bytes 1572872 | tf_op jit(solution)/shard_map/ppermute | solution.py:44
  101.4 0.8 copy-start.9
  102.2 11.3 %collective-permute-start.8 = (bf16[256,1,1024]{2,0,1:T(8,128)(2,1)S(1)}, bf16[256,1,1024]{2,0,1:T(8,128)(2,1)S(1)}, u32[]{:S(2)}, u32[]{:S(2)}) collective-permute-start(bf16[256,1,1024]{2,0,1:T(8,128)(2,1)S(1)} %collective-permute-done.7), channel_id=1, source_target_pairs={{0,1},{1,2},{2,3},{3,4},{4,5},{5,6},{6,7},{7,8},{8,9},{9,10},{10,1... | collective-permute-start | bytes 1572872 | tf_op jit(solution)/shard_map/ppermute | solution.py:44
  113.5 0.8 copy-start.11
  114.3 11.3 %collective-permute-start.9 = (bf16[256,1,1024]{2,0,1:T(8,128)(2,1)S(1)}, bf16[256,1,1024]{2,0,1:T(8,128)(2,1)S(1)}, u32[]{:S(2)}, u32[]{:S(2)}) collective-permute-start(bf16[256,1,1024]{2,0,1:T(8,128)(2,1)S(1)} %collective-permute-done.8), channel_id=1, source_target_pairs={{0,1},{1,2},{2,3},{3,4},{4,5},{5,6},{6,7},{7,8},{8,9},{9,10},{10,1... | collective-permute-start | bytes 1572872 | tf_op jit(solution)/shard_map/ppermute | solution.py:44
  125.6 0.8 copy-start.13
  126.4 11.3 %collective-permute-start.10 = (bf16[256,1,1024]{2,0,1:T(8,128)(2,1)S(1)}, bf16[256,1,1024]{2,0,1:T(8,128)(2,1)S(1)}, u32[]{:S(2)}, u32[]{:S(2)}) collective-permute-start(bf16[256,1,1024]{2,0,1:T(8,128)(2,1)S(1)} %collective-permute-done.9), channel_id=1, source_target_pairs={{0,1},{1,2},{2,3},{3,4},{4,5},{5,6},{6,7},{7,8},{8,9},{9,10},{10,1... | collective-permute-start | bytes 1572872 | tf_op jit(solution)/shard_map/ppermute | solution.py:44
  137.7 0.8 copy-start.15
  138.5 11.3 %collective-permute-start.11 = (bf16[256,1,1024]{2,0,1:T(8,128)(2,1)S(1)}, bf16[256,1,1024]{2,0,1:T(8,128)(2,1)S(1)}, u32[]{:S(2)}, u32[]{:S(2)}) collective-permute-start(bf16[256,1,1024]{2,0,1:T(8,128)(2,1)S(1)} %collective-permute-done.10), channel_id=1, source_target_pairs={{0,1},{1,2},{2,3},{3,4},{4,5},{5,6},{6,7},{7,8},{8,9},{9,10},{10,1... | collective-permute-start | bytes 1572872 | tf_op jit(solution)/shard_map/ppermute | solution.py:44
  149.8 0.8 copy-start.17
  150.5 11.4 %collective-permute-start.12 = (bf16[256,1,1024]{2,0,1:T(8,128)(2,1)S(1)}, bf16[256,1,1024]{2,0,1:T(8,128)(2,1)}, u32[]{:S(2)}, u32[]{:S(2)}) collective-permute-start(bf16[256,1,1024]{2,0,1:T(8,128)(2,1)S(1)} %collective-permute-done.11), channel_id=1, source_target_pairs={{0,1},{1,2},{2,3},{3,4},{4,5},{5,6},{6,7},{7,8},{8,9},{9,10},{10,1... | collective-permute-start | bytes 1572872 | tf_op jit(solution)/shard_map/ppermute | solution.py:44
  162.0 11.6 %collective-permute-start.13 = (bf16[256,1,1024]{2,0,1:T(8,128)(2,1)}, bf16[256,1,1024]{2,0,1:T(8,128)(2,1)}, u32[]{:S(2)}, u32[]{:S(2)}) collective-permute-start(bf16[256,1,1024]{2,0,1:T(8,128)(2,1)} %collective-permute-done.12), channel_id=1, source_target_pairs={{0,1},{1,2},{2,3},{3,4},{4,5},{5,6},{6,7},{7,8},{8,9},{9,10},{10,1... | collective-permute-start | bytes 1572872 | tf_op jit(solution)/shard_map/ppermute | solution.py:44
  162.0 37.4 %copy-start.18 = (bf16[256,1,1024]{2,0,1:T(8,128)(2,1)S(1)}, bf16[256,1,1024]{2,0,1:T(8,128)(2,1)}, u32[]{:S(2)}) copy-start(bf16[256,1,1024]{2,0,1:T(8,128)(2,1)} %copy-done.17) | copy-start | bytes 1572868
  162.0 37.5 %copy-start.16 = (bf16[256,1,1024]{2,0,1:T(8,128)(2,1)S(1)}, bf16[256,1,1024]{2,0,1:T(8,128)(2,1)}, u32[]{:S(2)}) copy-start(bf16[256,1,1024]{2,0,1:T(8,128)(2,1)} %copy-done.15) | copy-start | bytes 1572868
  162.0 37.5 %copy-start.14 = (bf16[256,1,1024]{2,0,1:T(8,128)(2,1)S(1)}, bf16[256,1,1024]{2,0,1:T(8,128)(2,1)}, u32[]{:S(2)}) copy-start(bf16[256,1,1024]{2,0,1:T(8,128)(2,1)} %copy-done.13) | copy-start | bytes 1572868
  162.0 37.6 %copy-start.12 = (bf16[256,1,1024]{2,0,1:T(8,128)(2,1)S(1)}, bf16[256,1,1024]{2,0,1:T(8,128)(2,1)}, u32[]{:S(2)}) copy-start(bf16[256,1,1024]{2,0,1:T(8,128)(2,1)} %copy-done.11) | copy-start | bytes 1572868
  162.0 37.6 %copy-start.10 = (bf16[256,1,1024]{2,0,1:T(8,128)(2,1)S(1)}, bf16[256,1,1024]{2,0,1:T(8,128)(2,1)}, u32[]{:S(2)}) copy-start(bf16[256,1,1024]{2,0,1:T(8,128)(2,1)} %copy-done.9) | copy-start | bytes 1572868
  162.0 37.7 %copy-start.8 = (bf16[256,1,1024]{2,0,1:T(8,128)(2,1)S(1)}, bf16[256,1,1024]{2,0,1:T(8,128)(2,1)}, u32[]{:S(2)}) copy-start(bf16[256,1,1024]{2,0,1:T(8,128)(2,1)} %copy-done.7) | copy-start | bytes 1572868
  162.0 37.7 %copy-start.6 = (bf16[256,1,1024]{2,0,1:T(8,128)(2,1)S(1)}, bf16[256,1,1024]{2,0,1:T(8,128)(2,1)}, u32[]{:S(2)}) copy-start(bf16[256,1,1024]{2,0,1:T(8,128)(2,1)} %copy-done.5) | copy-start | bytes 1572868
  162.0 37.8 %copy-start.4 = (bf16[256,1,1024]{2,0,1:T(8,128)(2,1)S(1)}, bf16[256,1,1024]{2,0,1:T(8,128)(2,1)}, u32[]{:S(2)}) copy-start(bf16[256,1,1024]{2,0,1:T(8,128)(2,1)} %copy-done.3) | copy-start | bytes 1572868
  173.6 11.5 %collective-permute-start.14 = (bf16[256,1,1024]{2,0,1:T(8,128)(2,1)}, bf16[256,1,1024]{2,0,1:T(8,128)(2,1)S(1)}, u32[]{:S(2)}, u32[]{:S(2)}) collective-permute-start(bf16[256,1,1024]{2,0,1:T(8,128)(2,1)} %collective-permute-done.13), channel_id=1, source_target_pairs={{0,1},{1,2},{2,3},{3,4},{4,5},{5,6},{6,7},{7,8},{8,9},{9,10},{10,1... | collective-permute-start | bytes 1572872 | tf_op jit(solution)/shard_map/ppermute | solution.py:44
  200.1 10.9 %copy-start.1 = (bf16[8192,1,1024]{2,0,1:T(8,128)(2,1)}, bf16[8192,1,1024]{2,0,1:T(8,128)(2,1)S(1)}, u32[]{:S(2)}) copy-start(bf16[8192,1,1024]{2,0,1:T(8,128)(2,1)S(1)} %constant_dynamic-update-slice_fusion) | copy-start | bytes 50331652
Sparse Core Ops, SparseCore 0:
  216.7 101.1 reduce-scatter.1
